TPU v7x, 256 devices: a whole 4x4x8 slice. The times are simulated.
256 devices in a mesh: ctx: 64 (over y_lo, z, x), wt: 4 (over y_hi, core).
Axes of the slice: x: 4, y: 4 (y_hi: 2, y_lo: 2; y = y_hi * 2 + y_lo), z: 8, core: 2. Of those that a mesh axis runs over, the one named last changes fastest.
Arguments:
- tokens: bfloat16 [32768, 4096], P('ctx'), may hold values from -6 to 6
- round_var: float32 [4096, 4096], P('ctx', 'wt'), may hold values from -6 to 6
- grid_base: bfloat16 [4096, 4096], P('ctx', 'wt'), may hold values from -8 to 7, as said below
- col_scale: float32 [4096], P('wt'), may hold values from 0.0015 to 0.006
- queries: bfloat16 [32768, 4096], P('ctx', 'wt'), may hold values from -4 to 4
- keys: bfloat16 [32768, 4096], P('ctx', 'wt'), may hold values from -4 to 4
- gates: bfloat16 [32768, 4096], P('ctx', 'wt'), may hold values from -6 to 6
- target: bfloat16 [32768, 4096], P('ctx', 'wt'), may hold values from -6 to 6
- decay_code: int32 [32], P('wt'), may hold values from 7 to 19
- boundary: int32 [128], P('ctx'), may hold values from 0 to 1, as said below
Outputs:
- gated_out: bfloat16 [32768, 4096], P('ctx', 'wt')
- rounding_grad: float32 [4096, 4096], P('ctx', 'wt')
Inputs may be any that keep to these rules, and one draw needn't show every extreme that they name: `grid_base`: integer grid levels. At least one group begins after a segment boundary.
All inputs are finite; a program needn't handle non-finite values.
Results may differ from a plain program's by a relative error of at most 0.011.
Values may be sent and summed in bfloat16 or wider, within the bound.
A program may use at most 128 MiB of HBM per device.

v0:
```python
import math
import jax
import jax.numpy as jnp
from jax import lax
from jax.sharding import PartitionSpec as P

HEADS = 32
HEAD = 128
GROUP = 256
epsilon = 1e-06
loss_weight = 1024.0


def carried_in(part, axis, combine, identity, reverse):
    count = lax.axis_size(axis)
    place = lax.axis_index(axis)
    ahead = count - 1 - place if reverse else place
    gathered = jax.tree.map(lambda a: lax.all_gather(a, axis), part)
    state = jax.tree.map(lambda a, e: jnp.zeros_like(a) + jnp.asarray(e, a.dtype), part, identity)

    def one(step, state):
        source = count - 1 - step if reverse else step
        return combine(
            state, jax.tree.map(lambda a: lax.dynamic_index_in_dim(a, source, 0, False), gathered)
        )

    return lax.fori_loop(0, ahead, one, state)


def combine(earlier, later):
    return (earlier[0] * later[0], later[0][:, None, None] * earlier[1] + later[1])


def tables(decay_code):
    decay_rate = jnp.exp2(-decay_code.astype(jnp.float32))
    offsets = jnp.arange(GROUP).astype(jnp.float32)
    query_decay = jnp.exp(-offsets[:, None] * decay_rate[None, :])
    key_decay = jnp.exp(-(GROUP - offsets)[:, None] * decay_rate[None, :])
    spacing = offsets[:, None] - offsets[None, :]
    causal_decay = jnp.where(
        spacing[None] >= 0.0,
        jnp.exp(-jnp.maximum(spacing, 0.0)[None] * decay_rate[:, None, None]),
        0.0,
    )
    group_decay = jnp.exp(-GROUP * decay_rate)
    return (query_decay, key_decay, causal_decay, group_decay)


def on_device(
    tokens, round_var, grid_base, col_scale, queries, keys, gates, target, decay_code, boundary
):
    squash = jax.nn.sigmoid(round_var)
    raw_level = 1.2 * squash - 0.1
    soft_part = jnp.clip(raw_level, 0.0, 1.0)
    slopes = jnp.where((raw_level > 0.0) & (raw_level < 1.0), 1.2 * squash * (1.0 - squash), 0.0)
    weight = (col_scale[None, :] * (grid_base.astype(jnp.float32) + soft_part)).astype(jnp.bfloat16)
    rows_here = tokens.shape[0]
    col_count = queries.shape[1]
    head_count = col_count // HEAD
    blocks = rows_here // GROUP
    ctx_count = lax.axis_size("ctx")
    projected = jnp.dot(
        tokens,
        lax.all_gather(weight, "ctx", axis=0, tiled=True),
        preferred_element_type=jnp.float32,
    )
    shape4 = (blocks, GROUP, head_count, HEAD)
    value_all = projected.astype(jnp.bfloat16).reshape(shape4)
    query_all = queries.reshape(shape4)
    key_all = keys.reshape(shape4)
    query_decay, key_decay, causal_decay, group_decay = tables(decay_code)
    scores = jnp.einsum("cihd,cjhd->chij", query_all, key_all, preferred_element_type=jnp.float32)
    weights = (scores * causal_decay[None]).astype(jnp.bfloat16)
    query_dec = (query_all * query_decay[None, :, :, None]).astype(jnp.bfloat16)
    key_dec = (key_all * key_decay[None, :, :, None]).astype(jnp.bfloat16)
    intra = jnp.einsum("chij,cjhe->cihe", weights, value_all, preferred_element_type=jnp.float32)
    updates = jnp.einsum("cjhd,cjhe->chde", key_dec, value_all, preferred_element_type=jnp.float32)
    multiplier = 1.0 - 0.5 * boundary.astype(jnp.float32)
    local_state = jnp.zeros((head_count, HEAD, HEAD), jnp.float32)
    state_coef = jnp.ones((head_count,), jnp.float32)
    local_list = []
    coef_list = []
    for block in range(blocks):
        state_coef = state_coef * multiplier[block]
        local_state = multiplier[block] * local_state
        local_list.append(local_state)
        coef_list.append(state_coef)
        local_state = group_decay[:, None, None] * local_state + updates[block]
        state_coef = state_coef * group_decay
    prefix = carried_in(
        (state_coef, local_state),
        "ctx",
        combine,
        (jnp.ones_like(state_coef), jnp.zeros_like(local_state)),
        False,
    )
    entering = prefix[1]
    states = jnp.stack(
        [
            part_state + part_coef[:, None, None] * entering
            for part_state, part_coef in zip(local_list, coef_list)
        ]
    )
    attn_all = intra + jnp.einsum(
        "cihd,chde->cihe",
        query_dec,
        states.astype(jnp.bfloat16),
        preferred_element_type=jnp.float32,
    )
    attn = attn_all.reshape(rows_here, col_count)
    row_squares = lax.psum(jnp.sum(attn * attn, axis=1), "wt")
    rms = jnp.sqrt(row_squares / (HEADS * HEAD) + epsilon)
    normed = attn / rms[:, None]
    gate_open = jax.nn.sigmoid(gates.astype(jnp.float32))
    gated = normed * gate_open
    gated_out = gated.astype(jnp.bfloat16)
    grad_gated = (gated - target.astype(jnp.float32)) * (
        loss_weight / math.sqrt(rows_here * ctx_count)
    )
    grad_normed = grad_gated * gate_open
    row_inner = lax.psum(jnp.sum(grad_normed * normed, axis=1), "wt")
    grad_attn = (
        (grad_normed - normed * (row_inner / (HEADS * HEAD))[:, None]) / rms[:, None]
    ).astype(jnp.bfloat16)
    grad_all = grad_attn.reshape(shape4)
    back_intra = jnp.einsum(
        "chij,cihe->cjhe", weights, grad_all, preferred_element_type=jnp.float32
    )
    collected = jnp.einsum(
        "cihd,cihe->chde", query_dec, grad_all, preferred_element_type=jnp.float32
    )
    later_local = jnp.zeros((head_count, HEAD, HEAD), jnp.float32)
    later_coef = jnp.ones((head_count,), jnp.float32)
    next_list = [None] * blocks
    next_coefs = [None] * blocks
    for block in reversed(range(blocks)):
        next_list[block] = later_local
        next_coefs[block] = later_coef
        later_local = multiplier[block] * (
            collected[block] + group_decay[:, None, None] * later_local
        )
        later_coef = later_coef * group_decay * multiplier[block]
    suffix = carried_in(
        (later_coef, later_local),
        "ctx",
        combine,
        (jnp.ones_like(later_coef), jnp.zeros_like(later_local)),
        True,
    )
    from_later = suffix[1]
    next_states = jnp.stack(
        [
            part_state + part_coef[:, None, None] * from_later
            for part_state, part_coef in zip(next_list, next_coefs)
        ]
    )
    grad_values = back_intra + jnp.einsum(
        "cjhd,chde->cjhe",
        key_dec,
        next_states.astype(jnp.bfloat16),
        preferred_element_type=jnp.float32,
    )
    grad_values = grad_values.astype(jnp.bfloat16).reshape(rows_here, col_count)
    full_term = lax.dot_general(
        tokens, grad_values, (((0,), (0,)), ((), ())), preferred_element_type=jnp.float32
    )
    weight_grad = lax.psum_scatter(full_term, "ctx", scatter_dimension=0, tiled=True)
    rounding_grad = col_scale[None, :] * slopes * weight_grad
    return (gated_out, rounding_grad)


def solution(mesh):
    placed = (
        P("ctx", None),
        P("ctx", "wt"),
        P("ctx", "wt"),
        P("wt"),
        P("ctx", "wt"),
        P("ctx", "wt"),
        P("ctx", "wt"),
        P("ctx", "wt"),
        P("wt"),
        P("ctx"),
    )
    return jax.shard_map(
        on_device,
        mesh=mesh,
        in_specs=placed,
        out_specs=(P("ctx", "wt"), P("ctx", "wt")),
        check_vma=False,
    )
```

profile of v0, /device:TPU:24, one launch (start us, length us, event | category | flops | bytes accessed | tf_op | source)
XLA Modules:
  0.0 1666.2 jit_solution(1325036017043877112)
XLA Ops:
  7.2 1.8 multiply_convert_fusion.7
  9.1 1.5 copy.66
  13.8 1.3 broadcast_multiply_fusion.1
  15.1 307.1 %all-gather.6.cloned.1.call-done = bf16[4096,1024]{1,0:T(8,128)(2,1)} async-done(((bf16[64,1024]{1,0:T(8,128)(2,1)}), bf16[4096,1024]{1,0:T(8,128)(2,1)}) %all-gather.6.cloned.1.call-update) | async-done | bytes 8388624 | tf_op jit(solution)/shard_map/all_gather | solution.py:64
  322.2 9.1 fusion
  332.6 1.3 fusion.11
  333.9 1.5 slice_add_fusion.1
  335.4 1.3 multiply_dynamic-update-slice_fusion
  336.7 160.3 %all-reduce.2 = (f32[512]{0:T(512)S(1)}, f32[512]{0:T(512)S(1)}) all-reduce(f32[512]{0:T(512)S(1)} %get-tuple-element.170, f32[512]{0:T(512)S(1)} %multiply_dynamic-update-slice_fusion), channel_id=2, replica_groups=mesh['ctx'=64,'wt'=4] {'ctx'}, use_global_device_ids=true, to_apply=%add | all-reduce | flops 1024 | bytes 8192
  497.1 1.5 copy.65
  498.6 1.5 copy.50
  502.6 2.1 fusion.34
  504.7 208.0 %all-gather.8.cloned.1.call-done = f32[64,8,128,128]{3,2,1,0:T(8,128)} async-done(((f32[1,8,128,128]{3,2,1,0:T(8,128)}), f32[64,8,128,128]{3,2,1,0:T(8,128)}) %all-gather.8.cloned.1.call-update) | async-done | bytes 33554448 | tf_op jit(solution)/shard_map/all_gather | solution.py:18
  712.8 39.4 %while.26 = (s32[]{:T(128)}, f32[8,128,128]{2,1,0:T(8,128)S(1)}, s32[]{:T(128)}, f32[64,8]{1,0:T(8,128)S(1)}, f32[64,8,128,128]{3,2,1,0:T(8,128)}, /*index=5*/s32[]{:T(128)}, s32[]{:T(128)}, s32[]{:T(128)}) while((s32[]{:T(128)}, f32[8,128,128]{2,1,0:T(8,128)S(1)}, s32[]{:T(128)}, f32[64,8]{1,0:T(8,128)S(1)}, f32[64,8,128,128]{3,2,1,0:T(8,128)}, ...), condition=%wide.region_1.2_spmd, body=%wide.region_0.1_spmd.sunk | while | flops 262149 | bytes 1573095 | solution.py:27
  712.8 1.2 bitcast_add_fusion.6
  715.3 1.2 bitcast_add_fusion.6
  717.7 1.2 bitcast_add_fusion.6
  721.4 1.2 bitcast_add_fusion.6
  725.1 1.2 bitcast_add_fusion.6
  731.3 1.2 bitcast_add_fusion.6
  735.0 1.2 bitcast_add_fusion.6
  738.6 1.2 bitcast_add_fusion.6
  741.1 1.2 bitcast_add_fusion.6
  744.8 1.2 bitcast_add_fusion.6
  748.5 1.2 bitcast_add_fusion.6
  752.2 2.5 fusion.27
  754.7 3.5 multiply_reduce_fusion.1
  758.1 7.1 psum.14
  765.3 3.0 copy.53
  768.3 3.0 multiply_reduce_fusion
  771.3 8.2 psum.15
  779.5 4.1 fusion.4
  786.3 2.1 fusion.12
  788.6 1.8 fusion.6
  790.4 406.6 %all-gather.10.cloned.1.call-done = f32[64,8,128,128]{3,2,1,0:T(8,128)} async-done(((f32[1,8,128,128]{3,2,1,0:T(8,128)}), f32[64,8,128,128]{3,2,1,0:T(8,128)}) %all-gather.10.cloned.1.call-update) | async-done | bytes 33554448 | tf_op jit(solution)/shard_map/all_gather | solution.py:18
  1197.0 38.3 %while.27 = (s32[]{:T(128)}, f32[8,128,128]{2,1,0:T(8,128)S(1)}, s32[]{:T(128)}, f32[64,8]{1,0:T(8,128)S(1)}, f32[64,8,128,128]{3,2,1,0:T(8,128)}, /*index=5*/s32[]{:T(128)}, s32[]{:T(128)}, s32[]{:T(128)}, s32[]{:T(128)}) while((s32[]{:T(128)}, f32[8,128,128]{2,1,0:T(8,128)S(1)}, s32[]{:T(128)}, f32[64,8]{1,0:T(8,128)S(1)}, ...), condition=%wide.region_7.8_spmd, body=%wide.region_6.7_spmd.sunk | while | flops 262150 | bytes 1573115 | solution.py:27
  1197.1 1.3 bitcast_add_fusion.7
  1212.0 1.2 bitcast_add_fusion.7
  1213.2 1.2 bitcast_add_fusion.7
  1214.5 1.2 bitcast_add_fusion.7
  1215.7 1.2 bitcast_add_fusion.7
  1216.9 1.2 bitcast_add_fusion.7
  1218.1 1.2 bitcast_add_fusion.7
  1235.4 1.9 fusion.29
  1238.8 10.4 convolution_bitcast_fusion
  1249.2 17.4 %copy.63 = f32[4096,1024]{1,0:T(8,128)} copy(f32[4096,1024]{0,1:T(8,128)} %convolution_bitcast_fusion) | data formatting | bytes 33554432
  1266.7 391.2 %reduce-scatter.4.cloned.1.call-done = f32[64,1024]{1,0:T(8,128)} async-done(((f32[4096,1024]{1,0:T(8,128)}), f32[64,1024]{1,0:T(8,128)}) %reduce-scatter.4.cloned.1.call-update) | async-done | bytes 262160 | tf_op jit(solution)/shard_map/reduce_scatter | solution.py:167
  1657.9 1.8 multiply_multiply_fusion.1
  (174 shorter events, 64.5 us)
Async XLA Ops:
  7.2 3.5 copy-start.15
  7.2 4.8 copy-start.14
  7.2 6.0 copy-start.13
  7.2 315.0 %all-gather.6.cloned.1.call-start = ((), (), s32[]{:S(2)}) async-start(), calls=%async_computation.1 | async-start | bytes 8519680 | tf_op jit(solution)/shard_map/all_gather | solution.py:64
  9.1 703.7 %all-gather.8.cloned.1.call-start = ((), (), s32[]{:S(2)}) async-start(), calls=%async_computation.2 | async-start | bytes 34078720 | tf_op jit(solution)/shard_map/all_gather | solution.py:18
  10.6 490.1 %copy-start = (bf16[64,8,8,128]{3,2,1,0:T(8,128)(2,1)}, bf16[64,8,8,128]{3,2,1,0:T(8,128)(2,1)S(1)}, u32[]{:S(2)}) copy-start(bf16[64,8,8,128]{3,2,1,0:T(8,128)(2,1)S(1)} %copy.66) | copy-start | bytes 3145732
  332.6 2.8 copy-start.5
  333.9 164.8 %copy-start.8 = (f32[2,8,128,128]{3,2,1,0:T(8,128)}, f32[2,8,128,128]{3,2,1,0:T(8,128)S(1)}, u32[]{:S(2)}) copy-start(f32[2,8,128,128]{3,2,1,0:T(8,128)S(1)} %fusion.11) | copy-start | bytes 3145732
  335.4 861.6 %all-gather.10.cloned.1.call-start = ((), (), s32[]{:S(2)}) async-start(), calls=%async_computation.3 | async-start | bytes 34078720 | tf_op jit(solution)/shard_map/all_gather | solution.py:18
  500.1 1.2 copy-start.2
  501.4 1.2 copy-start.6
  752.2 2.5 copy-start.3
  765.3 3.0 copy-start.10
  783.6 1.2 copy-start.4
  785.3 1.0 copy-start.9
  788.4 869.5 %reduce-scatter.4.cloned.1.call-start = ((), (), s32[]{:S(2)}) async-start(), calls=%async_computation.4 | async-start | bytes 17039360 | tf_op jit(solution)/shard_map/reduce_scatter | solution.py:167
  1197.0 40.2 %copy-start.7 = (f32[2,8,128,256]{3,2,1,0:T(8,128)S(1)}, f32[2,8,128,256]{3,2,1,0:T(8,128)}, u32[]{:S(2)}) copy-start(f32[2,8,128,256]{3,2,1,0:T(8,128)} %fusion.6) | copy-start | bytes 6291460
  1235.4 1.9 copy-start.1
  1266.6 391.3 %copy-start.11 = (f32[64,1024]{1,0:T(8,128)S(1)}, f32[64,1024]{1,0:T(8,128)}, u32[]{:S(2)}) copy-start(f32[64,1024]{1,0:T(8,128)} %param.15) | copy-start | bytes 786436
  1266.6 391.3 %copy-start.12 = (f32[1024]{0:T(1024)S(1)}, f32[1024]{0:T(1024)}, u32[]{:S(2)}) copy-start(f32[1024]{0:T(1024)} %param.17) | copy-start | bytes 12292
Sparse Core Ops, SparseCore 0:
  10.4 311.8 all-gather.5
  335.5 377.1 all-gather.7
  788.6 408.3 all-gather.9
  1266.8 391.0 reduce-scatter.3
where the time goes:
time: 1670 us
  waiting for transfers between devices  1310 us (78%)
  blocking collectives  176 us (11%)
  other arithmetic  97.5 us (6%)
  local copies, waits for them, and re-layouts  32.3 us (2%)
  matrix products  30.2 us (2%)
    all_gather x2, waiting for transfers between devices, carried_in(): gathered = jax.tree.map(lambda a: lax.all_gather(a, axis), part)  615 us
    reduce_scatter x1, waiting for transfers between devices, on_device(): lax.psum_scatter(full_term, 'ctx', scatter_dimension=0, tiled=True)  391 us
    all_gather x1, waiting for transfers between devices, on_device(): lax.all_gather(weight, 'ctx', axis=0, tiled=True)  307 us
    unnamed x1, blocking collectives  160 us
    add x63, other arithmetic, combine(): later[0][:, None, None] * earlier[1] + later[1]  75.1 us
  transfers between devices with their start and end apart: 4, of which 4 were waited for; matrix products, arithmetic and copies ran while one was open for 1% of the time, Pallas kernels for 0%

commit v1 on v0

--- a/solution.py
+++ b/solution.py
@@ -61,7 +61,9 @@
     ctx_count = lax.axis_size("ctx")
     projected = jnp.dot(
         tokens,
-        lax.all_gather(weight, "ctx", axis=0, tiled=True),
+        jnp.concatenate(
+            lax.all_to_all(jnp.stack([weight] * lax.axis_size("ctx")), "ctx", 0, 0), axis=0
+        ),
         preferred_element_type=jnp.float32,
     )
     shape4 = (blocks, GROUP, head_count, HEAD)

time: 1670 us -> 1560 us (0.934)
  waiting for transfers between devices: 1310 us -> 1180 us
    reduce_scatter x1 -> x0, waiting for transfers between devices: 391 us -> none  [on_device(): lax.psum_scatter(full_term, 'ctx', scatter_dimension=0, tiled=True)]
    unnamed x4, waiting for transfers between devices: 0.07 us -> 391 us
    all_gather x1 -> x0, waiting for transfers between devices: 307 us -> none  [on_device(): lax.all_gather(weight, 'ctx', axis=0, tiled=True)]
    all_to_all x0 -> x1, waiting for transfers between devices: none -> 178 us  [on_device(): lax.all_to_all(jnp.stack([weight] * lax.axis_size('ctx')), 'ctx', 0, 0)]
where the time goes in v1:
time: 1560 us
  waiting for transfers between devices  1180 us (76%)
  blocking collectives  176 us (11%)
  other arithmetic  95.9 us (6%)
  local copies, waits for them, and re-layouts  40.3 us (3%)
  matrix products  30.2 us (2%)
    all_gather x2, waiting for transfers between devices, carried_in(): gathered = jax.tree.map(lambda a: lax.all_gather(a, axis), part)  615 us
    unnamed x4, waiting for transfers between devices  391 us
    all_to_all x1, waiting for transfers between devices, on_device(): lax.all_to_all(jnp.stack([weight] * lax.axis_size('ctx')), 'ctx', 0, 0)  178 us
    unnamed x1, blocking collectives  161 us
    add x63, other arithmetic, combine(): later[0][:, None, None] * earlier[1] + later[1]  75.1 us
  transfers between devices with their start and end apart: 4, of which 4 were waited for; matrix products, arithmetic and copies ran while one was open for 1% of the time, Pallas kernels for 0%

profile of v1, /device:TPU:24, one launch (start us, length us, event | category | flops | bytes accessed | tf_op | source)
XLA Modules:
  0.0 1558.1 jit_solution(3448030889412618580)
XLA Ops:
  8.3 1.2 copy.46
  10.6 4.3 stack.20
  14.9 13.4 all-to-all-start
  32.2 1.4 broadcast_multiply_fusion.1
  33.7 177.7 %all-to-all-done = bf16[64,64,1024]{2,1,0:T(8,128)(2,1)} async-done(((bf16[64,64,1024]{2,1,0:T(8,128)(2,1)}), bf16[64,64,1024]{2,1,0:T(8,128)(2,1)}, u32[]{:S(2)}, u32[]{:S(2)}) %all-to-all-start) | async-done | bytes 8388640 | tf_op jit(solution)/shard_map/all_to_all | solution.py:65
  211.4 9.1 fusion
  221.7 1.3 fusion.11
  223.0 1.6 slice_add_fusion.1
  224.7 1.4 multiply_dynamic-update-slice_fusion
  226.0 161.1 %all-reduce.2 = (f32[512]{0:T(512)S(1)}, f32[512]{0:T(512)S(1)}) all-reduce(f32[512]{0:T(512)S(1)} %get-tuple-element.172, f32[512]{0:T(512)S(1)} %multiply_dynamic-update-slice_fusion), channel_id=2, replica_groups=mesh['ctx'=64,'wt'=4] {'ctx'}, use_global_device_ids=true, to_apply=%add | all-reduce | flops 1024 | bytes 8192
  387.2 1.5 copy.70
  388.7 1.5 copy.55
  392.7 2.1 fusion.34
  394.8 208.4 %all-gather.5.cloned.1.call-done = f32[64,8,128,128]{3,2,1,0:T(8,128)} async-done(((f32[1,8,128,128]{3,2,1,0:T(8,128)}), f32[64,8,128,128]{3,2,1,0:T(8,128)}) %all-gather.5.cloned.1.call-update) | async-done | bytes 33554448 | tf_op jit(solution)/shard_map/all_gather | solution.py:18
  603.3 39.7 %while.26 = (s32[]{:T(128)}, f32[8,128,128]{2,1,0:T(8,128)S(1)}, s32[]{:T(128)}, f32[64,8]{1,0:T(8,128)S(1)}, f32[64,8,128,128]{3,2,1,0:T(8,128)}, /*index=5*/s32[]{:T(128)}, s32[]{:T(128)}, s32[]{:T(128)}) while((s32[]{:T(128)}, f32[8,128,128]{2,1,0:T(8,128)S(1)}, s32[]{:T(128)}, f32[64,8]{1,0:T(8,128)S(1)}, f32[64,8,128,128]{3,2,1,0:T(8,128)}, ...), condition=%wide.region_1.2_spmd, body=%wide.region_0.1_spmd.sunk | while | flops 262149 | bytes 1573087 | solution.py:27
  608.2 1.2 bitcast_add_fusion.6
  610.7 1.2 bitcast_add_fusion.6
  613.2 1.2 bitcast_add_fusion.6
  615.7 1.2 bitcast_add_fusion.6
  618.1 1.2 bitcast_add_fusion.6
  620.6 1.2 bitcast_add_fusion.6
  631.7 1.2 bitcast_add_fusion.6
  634.2 1.2 bitcast_add_fusion.6
  636.7 1.2 bitcast_add_fusion.6
  639.1 1.2 bitcast_add_fusion.6
  641.6 1.2 bitcast_add_fusion.6
  643.0 2.6 fusion.27
  645.6 3.5 multiply_reduce_fusion.1
  649.1 3.0 copy.58
  652.1 7.1 psum.14
  659.2 3.0 multiply_reduce_fusion
  662.2 8.0 psum.15
  670.2 4.1 fusion.4
  677.0 2.2 fusion.12
  679.4 1.8 fusion.6
  681.3 406.8 %all-gather.7.cloned.1.call-done = f32[64,8,128,128]{3,2,1,0:T(8,128)} async-done(((f32[1,8,128,128]{3,2,1,0:T(8,128)}), f32[64,8,128,128]{3,2,1,0:T(8,128)}) %all-gather.7.cloned.1.call-update) | async-done | bytes 33554448 | tf_op jit(solution)/shard_map/all_gather | solution.py:18
  1088.1 38.5 %while.27 = (s32[]{:T(128)}, f32[8,128,128]{2,1,0:T(8,128)S(1)}, s32[]{:T(128)}, f32[64,8]{1,0:T(8,128)S(1)}, f32[64,8,128,128]{3,2,1,0:T(8,128)}, /*index=5*/s32[]{:T(128)}, s32[]{:T(128)}, s32[]{:T(128)}, s32[]{:T(128)}) while((s32[]{:T(128)}, f32[8,128,128]{2,1,0:T(8,128)S(1)}, s32[]{:T(128)}, f32[64,8]{1,0:T(8,128)S(1)}, ...), condition=%wide.region_7.8_spmd, body=%wide.region_6.7_spmd.sunk | while | flops 262150 | bytes 1573107 | solution.py:27
  1088.2 1.3 bitcast_add_fusion.7
  1093.3 1.2 bitcast_add_fusion.7
  1094.5 1.2 bitcast_add_fusion.7
  1095.7 1.2 bitcast_add_fusion.7
  1097.0 1.2 bitcast_add_fusion.7
  1098.2 1.2 bitcast_add_fusion.7
  1099.5 1.2 bitcast_add_fusion.7
  1126.7 2.0 fusion.29
  1130.2 10.4 convolution_bitcast_fusion
  1140.6 17.4 %copy.68 = f32[4096,1024]{1,0:T(8,128)} copy(f32[4096,1024]{0,1:T(8,128)} %convolution_bitcast_fusion) | data formatting | bytes 33554432
  1158.1 391.2 %reduce-scatter.4.cloned.1.call-done = f32[64,1024]{1,0:T(8,128)} async-done(((f32[4096,1024]{1,0:T(8,128)}), f32[64,1024]{1,0:T(8,128)}) %reduce-scatter.4.cloned.1.call-update) | async-done | bytes 262160
  (183 shorter events, 69.7 us)
Async XLA Ops:
  8.3 6.6 copy-start.10
  14.9 13.5 copy-start.13
  14.9 196.5 %all-to-all-start = ((bf16[64,64,1024]{2,1,0:T(8,128)(2,1)}), bf16[64,64,1024]{2,1,0:T(8,128)(2,1)}, u32[]{:S(2)}, u32[]{:S(2)}) async-start(bf16[64,64,1024]{2,1,0:T(8,128)(2,1)} %stack.20), calls=%async_computation | async-start | bytes 16777216 | tf_op jit(solution)/shard_map/all_to_all | solution.py:65
  28.3 0.7 copy-start.16
  28.3 2.0 copy-start.17
  28.3 3.3 copy-start.15
  28.3 574.9 %all-gather.5.cloned.1.call-start = ((), (), s32[]{:S(2)}) async-start(), calls=%async_computation.2 | async-start | bytes 34078720 | tf_op jit(solution)/shard_map/all_gather | solution.py:18
  28.9 361.9 %copy-start = (bf16[64,8,8,128]{3,2,1,0:T(8,128)(2,1)}, bf16[64,8,8,128]{3,2,1,0:T(8,128)(2,1)S(1)}, u32[]{:S(2)}) copy-start(bf16[64,8,8,128]{3,2,1,0:T(8,128)(2,1)S(1)} %copy.71) | copy-start | bytes 3145732
  221.7 2.9 copy-start.5
  223.0 165.7 %copy-start.8 = (f32[2,8,128,128]{3,2,1,0:T(8,128)}, f32[2,8,128,128]{3,2,1,0:T(8,128)S(1)}, u32[]{:S(2)}) copy-start(f32[2,8,128,128]{3,2,1,0:T(8,128)S(1)} %fusion.11) | copy-start | bytes 3145732
  224.6 863.5 %all-gather.7.cloned.1.call-start = ((), (), s32[]{:S(2)}) async-start(), calls=%async_computation.3 | async-start | bytes 34078720 | tf_op jit(solution)/shard_map/all_gather | solution.py:18
  390.2 1.2 copy-start.2
  391.4 1.2 copy-start.6
  643.0 2.6 copy-start.3
  649.1 10.1 copy-start.12
  674.3 1.2 copy-start.4
  676.0 1.0 copy-start.9
  679.3 870.0 %reduce-scatter.4.cloned.1.call-start = ((), (), s32[]{:S(2)}) async-start(), calls=%async_computation.4 | async-start | bytes 17039360
  1088.1 40.5 %copy-start.7 = (f32[2,8,128,256]{3,2,1,0:T(8,128)S(1)}, f32[2,8,128,256]{3,2,1,0:T(8,128)}, u32[]{:S(2)}) copy-start(f32[2,8,128,256]{3,2,1,0:T(8,128)} %fusion.6) | copy-start | bytes 6291460
  1126.7 2.0 copy-start.1
  1158.0 392.4 %copy-start.11 = (f32[64,1024]{0,1:T(8,128)S(1)}, f32[64,1024]{0,1:T(8,128)}, u32[]{:S(2)}) copy-start(f32[64,1024]{0,1:T(8,128)} %copy-done.10) | copy-start | bytes 786436
  1158.0 392.4 %copy-start.14 = (f32[1024]{0:T(1024)S(1)}, f32[1024]{0:T(1024)}, u32[]{:S(2)}) copy-start(f32[1024]{0:T(1024)} %param.17) | copy-start | bytes 12292
Sparse Core Ops, SparseCore 0:
  224.7 378.4 all-gather.4
  679.4 408.6 all-gather.6
  1158.2 391.0 reduce-scatter.3
